TPU v7x, 32 devices: a whole 2x2x4 slice. The times are simulated.
32 devices in a mesh: expert: 4 (over x, core), tensor: 4 (over z), kv: 2 (over y).
Axes of the slice: x: 2, y: 2, z: 4, core: 2. Of those that a mesh axis runs over, the one named last changes fastest.
Arguments:
- residual_stream: bfloat16 [1024, 4096], P('expert', ('tensor', 'kv')), may hold values from -13 to 13
- grad_output: bfloat16 [1024, 4096], P('expert', ('tensor', 'kv')), may hold values from -6 to 6
- norm_gain: bfloat16 [4096], P(('tensor', 'kv')), may hold values from 0.5 to 1.5
- expert_ids: int32 [1024, 2], P('expert'), may hold values from 0 to 3, all different within a row; in each aligned block of 256 rows (0 to 255, 256 to 511, ...) at most 160 rows name the same one
- gate_probs: float32 [1024, 2], P('expert'), may hold values from 0.1 to 0.9
- w_gate: bfloat16 [4, 14336, 4096], P('expert', ('tensor', 'kv')), may hold values from -0.125 to 0.125
- w_up: bfloat16 [4, 14336, 4096], P('expert', ('tensor', 'kv')), may hold values from -0.125 to 0.125
- w_down: bfloat16 [4, 14336, 4096], P('expert', ('tensor', 'kv')), may hold values from -0.046875 to 0.046875
Outputs:
- input_grad: bfloat16 [1024, 4096], P('expert', ('tensor', 'kv'))
Inputs may be any that keep to these rules, and one draw needn't show every extreme that they name: `expert_ids`: each row names two different experts. In each aligned block of 256 rows (the rows of one index of the expert axis) no expert is named by more than 160 rows, a bound that some block reaches.
All inputs are finite; a program needn't handle non-finite values.
Results may differ from a plain program's by a relative error of at most 0.018.
Values may be sent and summed in bfloat16 or wider, within the bound.
A program may use at most 128 MiB of HBM per device.

v0:
```python
import jax
import jax.numpy as jnp
from jax import lax
from jax.sharding import PartitionSpec as P

D = 4096
CAP = 160


epsilon = 1e-05
contract_width = (((1,), (1,)), ((), ()))
contract_hidden = (((0,), (1,)), ((), ()))
contract_slots = (((0,), (0,)), ((), ()))


def slot_matrix(ids_block, experts):
    flattened = ids_block.reshape(-1)
    onehot = (flattened[:, None] == jnp.arange(experts, dtype=jnp.int32)[None, :]).astype(jnp.int32)
    before = jnp.cumsum(onehot, axis=0) - onehot
    position = jnp.sum(before * onehot, axis=1)
    slot_index = flattened * CAP + position
    table = jnp.arange(experts * CAP, dtype=jnp.int32)
    return (slot_index[None, :] == table[:, None]).astype(jnp.bfloat16)


def shards(residual_stream, grad_output, norm_gain, expert_ids, gate_probs, w_gate, w_up, w_down):
    experts = lax.axis_size("expert")
    local_width = residual_stream.shape[1]
    tokens_here = residual_stream.shape[0]
    stream = residual_stream.astype(jnp.float32)
    squares = lax.psum(jnp.sum(stream * stream, axis=1), ("tensor", "kv"))
    inverse_rms = lax.rsqrt(squares / D + epsilon)[:, None]
    gains = norm_gain.astype(jnp.float32)
    normed = (stream * inverse_rms * gains).astype(jnp.bfloat16)
    table = slot_matrix(expert_ids, experts)
    repeated_x = jnp.repeat(normed, 2, axis=0)
    scaled = (
        jnp.repeat(grad_output.astype(jnp.float32), 2, axis=0) * gate_probs.reshape(-1, 1)
    ).astype(jnp.bfloat16)
    routed_x = jnp.dot(table, repeated_x, preferred_element_type=jnp.float32).astype(jnp.bfloat16)
    routed_grad = jnp.dot(table, scaled, preferred_element_type=jnp.float32).astype(jnp.bfloat16)
    routed_x = routed_x.reshape(experts, CAP, local_width)
    routed_grad = routed_grad.reshape(experts, CAP, local_width)
    gate_weight, up_weight, down_weight = (w_gate[0], w_up[0], w_down[0])
    pieces_x = lax.all_to_all(routed_x, "expert", split_axis=0, concat_axis=0, tiled=True)
    pieces_dy = lax.all_to_all(routed_grad, "expert", split_axis=0, concat_axis=0, tiled=True)
    full_x = lax.all_gather(pieces_x, ("tensor", "kv"), axis=2, tiled=True)
    full_dy = lax.all_gather(pieces_dy, ("tensor", "kv"), axis=2, tiled=True)
    leading = full_x.shape[0]
    items = full_x.shape[1]
    matrix_x = full_x.reshape(leading * items, D)
    matrix_dy = full_dy.reshape(leading * items, D)
    gate_value = lax.dot_general(
        matrix_x, gate_weight, contract_width, preferred_element_type=jnp.float32
    )
    up_value = lax.dot_general(
        matrix_x, up_weight, contract_width, preferred_element_type=jnp.float32
    )
    act_grad = lax.dot_general(
        matrix_dy, down_weight, contract_width, preferred_element_type=jnp.float32
    )
    sigmoid_gate = jax.nn.sigmoid(gate_value)
    activated = gate_value * sigmoid_gate
    gate_grad = (
        act_grad * up_value * sigmoid_gate * (1.0 + gate_value * (1.0 - sigmoid_gate))
    ).astype(jnp.bfloat16)
    up_grad = (act_grad * activated).astype(jnp.bfloat16)
    total = lax.dot_general(
        gate_weight, gate_grad, contract_hidden, preferred_element_type=jnp.float32
    )
    summed = lax.psum_scatter(
        total
        + lax.dot_general(up_weight, up_grad, contract_hidden, preferred_element_type=jnp.float32),
        ("tensor", "kv"),
        scatter_dimension=0,
        tiled=True,
    )
    returned = summed.T.astype(jnp.bfloat16).reshape(leading, items, local_width)
    combined = lax.all_to_all(returned, "expert", split_axis=0, concat_axis=0, tiled=True)
    gathered = lax.dot_general(
        table,
        combined.reshape(experts * CAP, local_width),
        contract_slots,
        preferred_element_type=jnp.float32,
    )
    token_grad = gathered.reshape(tokens_here, 2, local_width).sum(axis=1)
    scaled_grad = token_grad * gains
    projection = lax.psum(jnp.sum(scaled_grad * stream, axis=1), ("tensor", "kv"))[:, None]
    result = inverse_rms * scaled_grad - stream * inverse_rms**3 * projection / D
    return result.astype(jnp.bfloat16)


def solution(mesh):
    placed = (
        P("expert", ("tensor", "kv")),
        P("expert", ("tensor", "kv")),
        P(("tensor", "kv")),
        P("expert", None),
        P("expert", None),
        P("expert", ("tensor", "kv"), None),
        P("expert", ("tensor", "kv"), None),
        P("expert", ("tensor", "kv"), None),
    )
    return jax.shard_map(
        shards, mesh=mesh, in_specs=placed, out_specs=P("expert", ("tensor", "kv")), check_vma=False
    )
```

profile of v0, /device:TPU:0, one launch (start us, length us, event | category | flops | bytes accessed | tf_op | source)
XLA Modules:
  0.0 495.1 jit_solution(6443957624818157551)
XLA Ops:
  6.5 0.9 copy.15
  7.4 0.1 reshape.79
  7.7 1.2 reduce-window.6
  8.9 0.2 slice_reduce_fusion
  9.1 0.2 reduce-window.9
  9.4 0.8 copy.18
  10.3 0.1 mul.103
  10.4 1.2 broadcast_in_dim.4
  11.6 0.7 reshape.81
  12.4 0.6 convolution_convert_fusion.1
  12.9 14.4 %all_to_all.15 = bf16[4,160,512]{2,1,0:T(8,128)(2,1)} all-to-all(bf16[4,160,512]{2,1,0:T(8,128)(2,1)S(1)} %bitcast.69), channel_id=1, replica_groups=mesh['expert'=4,'tensor'=4,'kv'=2] {'expert'}, dimensions={0} | all-to-all | bytes 1310720 | tf_op jit(solution)/shard_map/all_to_all | solution.py:46
  27.5 22.7 %psum.14 = f32[256]{0:T(256)S(1)} all-reduce(f32[256]{0:T(256)S(1)} %fusion.27), channel_id=1, replica_groups=mesh['expert'=4,'tensor'=4,'kv'=2] {'tensor','kv'}, use_global_device_ids=true, to_apply=%region_1.0 | all-reduce | flops 256 | bytes 2048 | tf_op jit(solution)/shard_map/psum | solution.py:31
  50.4 0.3 broadcast_in_dim.5
  50.7 0.2 reshape.84
  50.9 0.5 convolution_convert_fusion
  51.4 13.3 %all_to_all.16 = bf16[4,160,512]{2,1,0:T(8,128)(2,1)} all-to-all(bf16[4,160,512]{2,1,0:T(8,128)(2,1)S(1)} %bitcast.70), channel_id=1, replica_groups=mesh['expert'=4,'tensor'=4,'kv'=2] {'expert'}, dimensions={0} | all-to-all | bytes 1310720 | tf_op jit(solution)/shard_map/all_to_all | solution.py:45
  64.7 0.2 reduce-scatter.2.cloned.1.call-start
  65.0 50.3 %all-gather.3.cloned.1.call-done = bf16[4,160,4096]{2,1,0:T(8,128)(2,1)} async-done(((bf16[4,160,512]{2,1,0:T(8,128)(2,1)}), bf16[4,160,4096]{2,1,0:T(8,128)(2,1)}) %all-gather.3.cloned.1.call-update) | async-done | bytes 5242896 | tf_op jit(solution)/shard_map/all_gather | solution.py:48
  115.2 15.9 %fusion.8 = f32[640,1792]{1,0:T(8,128)} fusion(bf16[640,4096]{1,0:T(8,128)(2,1)} %bitcast.72, bf16[1,1792,4096]{2,1,0:T(8,128)(2,1)} %param.15), kind=kOutput, calls=%fused_computation.8 | convolution fusion | flops 9395240960 | bytes 24510464 | tf_op jit(solution)/shard_map/dot_general | solution.py:59
  131.1 71.2 %all-gather.5.cloned.1.call-done = bf16[4,160,4096]{2,1,0:T(8,128)(2,1)} async-done(((bf16[4,160,512]{2,1,0:T(8,128)(2,1)}), bf16[4,160,4096]{2,1,0:T(8,128)(2,1)}) %all-gather.5.cloned.1.call-update) | async-done | bytes 5242896 | tf_op jit(solution)/shard_map/all_gather | solution.py:47
  202.3 16.1 %fusion.2 = f32[640,1792]{1,0:T(8,128)} fusion(bf16[640,4096]{1,0:T(8,128)(2,1)} %bitcast.73, bf16[1,1792,4096]{2,1,0:T(8,128)(2,1)} %param.13), kind=kOutput, calls=%fused_computation.2 | convolution fusion | flops 9395240960 | bytes 24510464 | tf_op jit(solution)/shard_map/dot_general | solution.py:53
  218.4 21.7 %multiply_convert_fusion.1.clone.4 = bf16[640,1792]{1,0:T(8,128)(2,1)} fusion(f32[640,1792]{1,0:T(8,128)} %fusion.2, f32[640,1792]{1,0:T(8,128)} %fusion.8, bf16[640,4096]{1,0:T(8,128)(2,1)S(1)} %bitcast.74, bf16[1,1792,4096]{2,1,0:T(8,128)(2,1)} %param.14), kind=kOutput, calls=%fused_computation.12.clone.clone.clone.1 | convolution fusion | flops 9406709760 | bytes 31391744 | tf_op jit(solution)/shard_map/dot_general | solution.py:56
  240.1 16.2 %fusion = f32[640,4096]{1,0:T(8,128)} fusion(bf16[1,1792,4096]{2,1,0:T(8,128)(2,1)} %param.13, bf16[640,1792]{1,0:T(8,128)(2,1)} %multiply_convert_fusion.1.clone.4), kind=kOutput, calls=%fused_computation | convolution fusion | flops 9395240960 | bytes 27459584 | tf_op jit(solution)/shard_map/dot_general | solution.py:68
  256.3 18.3 %add_bitcast_fusion = f32[4096,640]{0,1:T(8,128)} fusion(f32[640,4096]{1,0:T(8,128)} %fusion, bf16[1,1792,4096]{2,1,0:T(8,128)(2,1)} %param.14, f32[640,1792]{1,0:T(8,128)S(1)} %copy-done.4, f32[640,1792]{1,0:T(8,128)} %fusion.2), kind=kOutput, calls=%fused_computation.10 | convolution fusion | flops 9404743680 | bytes 44826624 | tf_op jit(solution)/shard_map/dot_general | solution.py:73
  274.6 176.9 %reduce-scatter.2.cloned.1.call-done = f32[512,640]{0,1:T(8,128)} async-done(((f32[4096,640]{0,1:T(8,128)}), f32[512,640]{0,1:T(8,128)}) %reduce-scatter.2.cloned.1.call-update) | async-done | bytes 1310736 | tf_op jit(solution)/shard_map/reduce_scatter | solution.py:71
  451.6 2.2 convert_element_type.55
  453.8 3.5 all-to-all-start.2
  457.5 10.0 %all-to-all-done.2 = bf16[4,160,512]{2,1,0:T(8,128)(2,1)S(1)} async-done(((bf16[4,160,512]{2,1,0:T(8,128)(2,1)}), bf16[4,160,512]{2,1,0:T(8,128)(2,1)S(1)}, u32[]{:S(2)}, u32[]{:S(2)}) %all-to-all-start.2) | async-done | bytes 655392 | tf_op jit(solution)/shard_map/all_to_all | solution.py:79
  467.5 0.6 fusion.21
  468.1 0.2 fusion.34
  468.3 19.4 %psum.15 = f32[256]{0:T(256)S(1)} all-reduce(f32[256]{0:T(256)S(1)} %fusion.34), channel_id=1, replica_groups=mesh['expert'=4,'tensor'=4,'kv'=2] {'tensor','kv'}, use_global_device_ids=true, to_apply=%region_8.9 | all-reduce | flops 256 | bytes 2048 | tf_op jit(solution)/shard_map/psum | solution.py:88
  487.7 0.9 fusion.33
  (27 shorter events, 0.9 us)
Async XLA Ops:
  6.5 20.8 %copy-start.2 = (bf16[512]{0:T(512)(128)(2,1)S(1)}, bf16[512]{0:T(512)(128)(2,1)}, u32[]{:S(2)}) copy-start(bf16[512]{0:T(512)(128)(2,1)} %param.10) | copy-start | bytes 3076
  6.5 20.9 %copy-start = (bf16[256,512]{1,0:T(8,128)(2,1)S(1)}, bf16[256,512]{1,0:T(8,128)(2,1)}, u32[]{:S(2)}) copy-start(bf16[256,512]{1,0:T(8,128)(2,1)} %param.8) | copy-start | bytes 786436
  6.5 108.7 %all-gather.3.cloned.1.call-start = ((), (), s32[]{:S(2)}) async-start(), calls=%async_computation.4 | async-start | bytes 5898240 | tf_op jit(solution)/shard_map/all_gather | solution.py:48
  27.3 174.9 %all-gather.5.cloned.1.call-start = ((), (), s32[]{:S(2)}) async-start(), calls=%async_computation.5 | async-start | bytes 5898240 | tf_op jit(solution)/shard_map/all_gather | solution.py:47
  64.7 386.8 %reduce-scatter.2.cloned.1.call-start = ((), (), s32[]{:S(2)}) async-start(), calls=%async_computation.6 | async-start | bytes 11796480 | tf_op jit(solution)/shard_map/reduce_scatter | solution.py:71
  202.3 16.1 %copy-start.3 = (bf16[4,160,4096]{2,1,0:T(8,128)(2,1)S(1)}, bf16[4,160,4096]{2,1,0:T(8,128)(2,1)}, u32[]{:S(2)}) copy-start(bf16[4,160,4096]{2,1,0:T(8,128)(2,1)} %all-gather.5.cloned.1.call-done) | copy-start | bytes 15728644
  240.1 16.2 %copy-start.4 = (f32[640,1792]{1,0:T(8,128)S(1)}, f32[640,1792]{1,0:T(8,128)}, u32[]{:S(2)}) copy-start(f32[640,1792]{1,0:T(8,128)} %fusion.8) | copy-start | bytes 13762564
  274.6 182.9 %copy-start.1 = (s32[256,2]{0,1:T(2,128)S(1)}, s32[256,2]{0,1:T(2,128)}, u32[]{:S(2)}) copy-start(s32[256,2]{0,1:T(2,128)} %param.11) | copy-start | bytes 6148
  453.8 13.7 %all-to-all-start.2 = ((bf16[4,160,512]{2,1,0:T(8,128)(2,1)}), bf16[4,160,512]{2,1,0:T(8,128)(2,1)S(1)}, u32[]{:S(2)}, u32[]{:S(2)}) async-start(bf16[4,160,512]{2,1,0:T(8,128)(2,1)} %bitcast.11), calls=%async_computation.3 | async-start | bytes 1310720 | tf_op jit(solution)/shard_map/all_to_all | solution.py:79
Sparse Core Ops, SparseCore 0:
  27.5 87.7 all-gather.2
  117.3 84.9 all-gather.4
  274.8 176.7 reduce-scatter.1
where the time goes:
time: 496 us; the launch traced here: 495 us
  waiting for transfers between devices  308 us (62%)
  matrix products  89.9 us (18%)
  blocking collectives  69.8 us (14%)
  between operations  13.3 us (3%)
  other arithmetic  5.1 us (1%)
    reduce_scatter x1, waiting for transfers between devices, shards(): lax.psum_scatter(total + lax.dot_general(up_weight, up_grad, contract_hid...  177 us
    all_gather x1, waiting for transfers between devices, shards(): full_x = lax.all_gather(pieces_x, ('tensor', 'kv'), axis=2, tiled=True)  71.2 us
    all_gather x1, waiting for transfers between devices, shards(): full_dy = lax.all_gather(pieces_dy, ('tensor', 'kv'), axis=2, tiled=True)  50.3 us
    psum x1, blocking collectives, shards(): squares = lax.psum(jnp.sum(stream * stream, axis=1), ('tensor', 'kv'))  22.7 us
    dot_general x1, matrix products, shards(): lax.dot_general(matrix_x, up_weight, contract_width, preferred_element_ty...  21.7 us
    psum x1, blocking collectives, shards(): lax.psum(jnp.sum(scaled_grad * stream, axis=1), ('tensor', 'kv'))[:, None]  19.4 us
    dot_general x1, matrix products, shards(): lax.dot_general(up_weight, up_grad, contract_hidden, preferred_element_ty...  18.3 us
    dot_general x1, matrix products, shards(): lax.dot_general(gate_weight, gate_grad, contract_hidden, preferred_elemen...  16.2 us
  transfers between devices with their start and end apart: 4, of which 4 were waited for; matrix products, arithmetic and copies ran while one was open for 4% of the time, Pallas kernels for 0%

commit v1 on v0

--- a/solution.py
+++ b/solution.py
@@ -1,6 +1,10 @@
+import functools
+
 import jax
 import jax.numpy as jnp
 from jax import lax
+from jax.experimental import pallas as pl
+from jax.experimental.pallas import tpu as pltpu
 from jax.sharding import PartitionSpec as P
 
 D = 4096
@@ -90,6 +94,435 @@
     return result.astype(jnp.bfloat16)
 
 
+MESH = pl.DeviceIdType.MESH
+TILE = 256
+
+
+def fused_kernel(
+    T, x_ref, dy_ref, gain_ref, meta_ref, wg_ref, wu_ref, wd_ref, out_ref,
+    tok, acc, wbuf, hid, routed, crecv, xrecv, yrecv, zrecv, gains, metas, sel, prob,
+    ssq, own_sq, psend, precv,
+    ag_send, ag_recv, rs_send, rs_recv, small_send, small_recv, wsem, lsem,
+):
+    e = lax.axis_index("expert")
+    z = lax.axis_index("tensor")
+    y = lax.axis_index("kv")
+    core = e + 1 - 2 * lax.rem(e, 2)
+    across = lax.rem(e + 2, 4)
+    width = x_ref.shape[1]
+    hidden = wg_ref.shape[0]
+    tiles = hidden // TILE
+    blocks = 2 * T
+    inputs = (x_ref, dy_ref)
+
+    def z_of(d):
+        return lax.rem(z + T - d, T)
+
+    def y_of(s):
+        return y if s == 0 else 1 - y
+
+    def fb_of(d, s):
+        return z_of(d) * 2 + y_of(s)
+
+    def b_of(u, c):
+        base = core if c else e
+        return lax.rem(base + 2 * u, 4)
+
+    def slot(a, d, s, u, c):
+        return tok.at[a, fb_of(d, s), b_of(u, c)]
+
+    def number(a, d, s, u, c):
+        return (((a * T + d) * 2 + s) * 2 + u) * 2 + c
+
+    def plan(a, d, s, u, c):
+        if c:
+            return (d, s, u, 0), (core, z, y)
+        if a == 0:
+            if u:
+                return (d, s, 0, 0), (across, z, y)
+            if s:
+                return (d, 0, 0, 0), (e, z, 1 - y)
+        else:
+            if s:
+                return (d, 0, u, 0), (e, z, 1 - y)
+            if u:
+                return (d, 0, 0, 0), (across, z, y)
+        return (0, 0, 0, 0), (e, lax.rem(z + d, T), y)
+
+    def gather_copy(a, d, s, u, c):
+        source, target = plan(a, d, s, u, c)
+        n = number(a, d, s, u, c)
+        fb, b = fb_of(*source[:2]), b_of(*source[2:])
+        src = inputs[a] if source == (0, 0, 0, 0) else tok.at[a, fb, b]
+        return pltpu.make_async_remote_copy(
+            src_ref=src, dst_ref=tok.at[a, fb, b],
+            send_sem=ag_send.at[n], recv_sem=ag_recv.at[n],
+            device_id=target, device_id_type=MESH,
+        )
+
+    def gather_wait(a, d, s, u, c):
+        n = number(a, d, s, u, c)
+        here = slot(a, d, s, u, c)
+        pltpu.make_async_remote_copy(
+            src_ref=here, dst_ref=here, send_sem=ag_send.at[n], recv_sem=ag_recv.at[n],
+            device_id=plan(a, d, s, u, c)[1], device_id_type=MESH,
+        ).wait_recv()
+
+    steps = [(d, s) for d in range(T) for s in (0, 1)]
+    back = [(d, s) for d in list(range(1, T)) + [0] for s in (1, 0)]
+
+    def weight_copies(step):
+        if step < blocks:
+            fb, refs = fb_of(*steps[step]), (wg_ref, wu_ref, wd_ref)
+        else:
+            fb, refs = fb_of(*back[step - blocks]), (wg_ref, wu_ref)
+        columns = pl.ds(pl.multiple_of(fb * width, width), width)
+        return [
+            pltpu.make_async_copy(ref.at[:, columns], wbuf.at[step % 2, k], wsem.at[step % 2, k])
+            for k, ref in enumerate(refs)
+        ]
+
+    for copy in weight_copies(0):
+        copy.start()
+    local = [
+        pltpu.make_async_copy(x_ref, tok.at[0, fb_of(0, 0), e], lsem.at[0]),
+        pltpu.make_async_copy(dy_ref, tok.at[1, fb_of(0, 0), e], lsem.at[1]),
+        pltpu.make_async_copy(gain_ref, gains.at[fb_of(0, 0)], lsem.at[2]),
+        pltpu.make_async_copy(meta_ref, metas.at[e], lsem.at[3]),
+    ]
+    for copy in local:
+        copy.start()
+
+    peers = [(e, lax.rem(z + d, T), y_of(s)) for d in range(T) for s in (0, 1) if d or s]
+    sources = [fb_of(d, s) for d in range(T) for s in (0, 1) if d or s]
+    others = [(lax.rem(e + k, 4), z, y) for k in (1, 2, 3)]
+    barrier = pltpu.get_barrier_semaphore()
+    for peer in peers + others:
+        pl.semaphore_signal(barrier, inc=1, device_id=peer, device_id_type=MESH)
+    pl.semaphore_wait(barrier, len(peers) + len(others))
+
+    def remote(src, dst, send, recv, peer):
+        return pltpu.make_async_remote_copy(
+            src_ref=src, dst_ref=dst, send_sem=send, recv_sem=recv,
+            device_id=peer, device_id_type=MESH,
+        )
+
+    small = []
+    for k, peer in enumerate(others):
+        copy = remote(meta_ref, metas.at[e], small_send.at[k], small_recv.at[k], peer)
+        copy.start()
+        there = metas.at[lax.rem(e + 3 - k, 4)]
+        small.append((copy, remote(there, there, small_send.at[k], small_recv.at[k], peer)))
+    for d in range(1, T):
+        for a in (0, 1):
+            gather_copy(a, d, 0, 0, 0).start()
+    for k, peer in enumerate(peers):
+        n = 3 + k
+        copy = remote(gain_ref, gains.at[fb_of(0, 0)], small_send.at[n], small_recv.at[n], peer)
+        copy.start()
+        there = gains.at[sources[k]]
+        small.append((copy, remote(there, there, small_send.at[n], small_recv.at[n], peer)))
+
+    def level1(d):
+        if d:
+            gather_wait(0, d, 0, 0, 0)
+        gather_copy(0, d, 1, 0, 0).start()
+        gather_copy(0, d, 0, 1, 0).start()
+        gather_copy(0, d, 0, 0, 1).start()
+        if d:
+            gather_wait(1, d, 0, 0, 0)
+        gather_copy(1, d, 0, 1, 0).start()
+        gather_copy(1, d, 1, 0, 0).start()
+        gather_copy(1, d, 0, 0, 1).start()
+
+    def level2(d):
+        gather_wait(0, d, 1, 0, 0)
+        gather_copy(0, d, 1, 1, 0).start()
+        gather_copy(0, d, 1, 0, 1).start()
+        gather_wait(1, d, 0, 1, 0)
+        gather_copy(1, d, 1, 1, 0).start()
+        gather_copy(1, d, 0, 1, 1).start()
+
+    def level3(d):
+        gather_wait(0, d, 0, 1, 0)
+        gather_copy(0, d, 0, 1, 1).start()
+        gather_wait(1, d, 1, 0, 0)
+        gather_copy(1, d, 1, 0, 1).start()
+        gather_wait(0, d, 1, 1, 0)
+        gather_copy(0, d, 1, 1, 1).start()
+        gather_wait(1, d, 1, 1, 0)
+        gather_copy(1, d, 1, 1, 1).start()
+
+    def multiply(step):
+        d, s = steps[step]
+        for copy in weight_copies(step + 1):
+            copy.start()
+        for a in (0, 1):
+            for u in (0, 1):
+                gather_wait(a, d, s, u, 1)
+        fb = fb_of(d, s)
+        gain_row = gains[fb, 0:1, :]
+        mine = tok[0, fb, e].astype(jnp.float32)
+        own_sq[...] += jnp.sum(mine * mine, axis=1, keepdims=True)
+        for b in range(4):
+            rows = pl.ds(b * CAP, CAP)
+            picked = jnp.dot(sel[b], tok[0, fb, b], preferred_element_type=jnp.float32)
+            ssq[rows, :] += jnp.sum(picked * picked, axis=1, keepdims=True)
+            routed[0, rows, :] = (picked * gain_row).astype(jnp.bfloat16)
+            picked = jnp.dot(sel[b], tok[1, fb, b], preferred_element_type=jnp.float32)
+            routed[1, rows, :] = (picked * prob[rows, :]).astype(jnp.bfloat16)
+        for copy in weight_copies(step):
+            copy.wait()
+
+        def tile(n, carry):
+            rows = pl.ds(pl.multiple_of(n * TILE, TILE), TILE)
+            for k in range(3):
+                term = lax.dot_general(
+                    routed[k // 2], wbuf[step % 2, k, rows, :], contract_width,
+                    preferred_element_type=jnp.float32,
+                )
+                if step == 0:
+                    acc[k, n] = term
+                else:
+                    acc[k, n] += term
+            return carry
+
+        lax.fori_loop(0, tiles, tile, 0)
+
+    level1(0)
+    for copy in local:
+        copy.wait()
+    for copy, arrival in small[:3]:
+        arrival.wait_recv()
+    own_sq[...] = jnp.zeros_like(own_sq)
+    ssq[...] = jnp.zeros_like(ssq)
+    for b in range(4):
+        slots = metas[b, pl.ds(e, 1), :]
+        probs = metas[b, pl.ds(4 + e, 1), :]
+        index = lax.broadcasted_iota(jnp.int32, (CAP, slots.shape[1]), 0).astype(jnp.float32)
+        chosen = jnp.where(index == slots, 1.0, 0.0)
+        sel[b] = chosen.astype(jnp.bfloat16)
+        prob[pl.ds(b * CAP, CAP), :] = jnp.sum(chosen * probs, axis=1, keepdims=True)
+    for copy, arrival in small[3:]:
+        arrival.wait_recv()
+    level1(1)
+    level2(0)
+    level1(2)
+    level3(0)
+    level2(1)
+    level1(3)
+    multiply(0)
+    level3(1)
+    level2(2)
+    multiply(1)
+    level2(3)
+    level3(2)
+    multiply(2)
+    multiply(3)
+    level3(3)
+    for step in range(4, blocks):
+        multiply(step)
+    for a in (0, 1):
+        for n in range(1, blocks * 4):
+            c, u, s, d = n % 2, n // 2 % 2, n // 4 % 2, n // 8
+            gather_copy(a, d, s, u, c).wait_send()
+    for copy, arrival in small:
+        copy.wait_send()
+
+    inverse = lax.rsqrt(ssq[...] / D + epsilon)
+
+    def activate(n, carry):
+        columns = pl.ds(pl.multiple_of(n * TILE, TILE), TILE)
+        gate_value = acc[0, n] * inverse
+        up_value = acc[1, n] * inverse
+        act_grad = acc[2, n]
+        sigmoid_gate = jax.nn.sigmoid(gate_value)
+        hid[0, :, columns] = (
+            act_grad * up_value * sigmoid_gate * (1.0 + gate_value * (1.0 - sigmoid_gate))
+        ).astype(jnp.bfloat16)
+        hid[1, :, columns] = (act_grad * gate_value * sigmoid_gate).astype(jnp.bfloat16)
+        return carry
+
+    lax.fori_loop(0, tiles, activate, 0)
+
+    def core_copy(i, u):
+        return remote(
+            tok.at[0, i, lax.rem(core + 2 * u, 4)], crecv.at[i, u],
+            rs_send.at[i, u], rs_recv.at[i, u], (core, z, y),
+        )
+
+    def across_copy(i):
+        return remote(tok.at[1, i, 0], xrecv.at[i], rs_send.at[i, 2], rs_recv.at[i, 2], (across, z, y))
+
+    def pair_copy(i):
+        d = back[i][0]
+        return remote(tok.at[1, i, 1], yrecv.at[d], rs_send.at[i, 3], rs_recv.at[i, 3], (e, z, 1 - y))
+
+    def line_copy(i):
+        d = back[i][0]
+        return remote(
+            tok.at[1, i, 2], zrecv.at[d - 1], rs_send.at[i, 4], rs_recv.at[i, 4], (e, z_of(d), y)
+        )
+
+    def produce(i):
+        step = blocks + i
+        if i + 1 < blocks:
+            for copy in weight_copies(step + 1):
+                copy.start()
+        for copy in weight_copies(step):
+            copy.wait()
+
+        def tile(n, carry):
+            columns = pl.ds(pl.multiple_of(n * TILE, TILE), TILE)
+            total = jnp.dot(
+                hid[0], wbuf[step % 2, 0, :, columns], preferred_element_type=jnp.float32
+            ) + jnp.dot(hid[1], wbuf[step % 2, 1, :, columns], preferred_element_type=jnp.float32)
+            rounded = total.astype(jnp.bfloat16)
+            for b in range(4):
+                tok[0, i, b, :, columns] = lax.dot_general(
+                    sel[b], rounded[b * CAP : (b + 1) * CAP], contract_slots,
+                    preferred_element_type=jnp.float32,
+                ).astype(jnp.bfloat16)
+            return carry
+
+        lax.fori_loop(0, width // TILE, tile, 0)
+        core_copy(i, 1).start()
+        core_copy(i, 0).start()
+
+    def combine_cores(i):
+        core_copy(i, 1).wait_recv()
+        tok[1, i, 0] = (
+            tok[0, i, across].astype(jnp.float32) + crecv[i, 1].astype(jnp.float32)
+        ).astype(jnp.bfloat16)
+        across_copy(i).start()
+
+    def combine_across(i):
+        d, s = back[i]
+        core_copy(i, 0).wait_recv()
+        across_copy(i).wait_recv()
+        value = (
+            tok[0, i, e].astype(jnp.float32)
+            + crecv[i, 0].astype(jnp.float32)
+            + xrecv[i].astype(jnp.float32)
+        )
+        if s:
+            tok[1, i, 1] = value.astype(jnp.bfloat16)
+            pair_copy(i).start()
+            return None
+        pair_copy(i - 1).wait_recv()
+        value = value + yrecv[d].astype(jnp.float32)
+        if d:
+            tok[1, i, 2] = value.astype(jnp.bfloat16)
+            line_copy(i).start()
+            return None
+        return value
+
+    value = None
+    for i in range(blocks + 2):
+        if i < blocks:
+            produce(i)
+        if 1 <= i <= blocks:
+            combine_cores(i - 1)
+        if i >= 2:
+            value = combine_across(i - 2)
+    for i in range(blocks):
+        if back[i][1] == 0 and back[i][0]:
+            line_copy(i).wait_recv()
+            value = value + zrecv[back[i][0] - 1].astype(jnp.float32)
+
+    gain_row = gains[fb_of(0, 0), 0:1, :]
+    stream = x_ref[...].astype(jnp.float32)
+    scaled = value * gain_row
+    share = jnp.sum(scaled * stream, axis=1, keepdims=True)
+    tokens = stream.shape[0]
+    psend[...] = jnp.broadcast_to(share, (tokens, 128)).T[0:8, :]
+    final = []
+    for k, peer in enumerate(peers):
+        n = 3 + len(peers) + k
+        copy = remote(psend, precv.at[k], small_send.at[n], small_recv.at[n], peer)
+        copy.start()
+        final.append(copy)
+    inverse = lax.rsqrt(own_sq[...] / D + epsilon)
+    row = psend[...]
+    for k, copy in enumerate(final):
+        copy.wait_recv()
+        row = row + precv[k]
+    projection = jnp.broadcast_to(row[0:1, :], (128, tokens)).T[:, 0:1]
+    out_ref[...] = (
+        inverse * scaled - stream * (inverse * inverse * inverse * projection / D)
+    ).astype(out_ref.dtype)
+    for copy in final:
+        copy.wait_send()
+    for i in range(blocks):
+        core_copy(i, 0).wait_send()
+        core_copy(i, 1).wait_send()
+        across_copy(i).wait_send()
+        if back[i][1]:
+            pair_copy(i).wait_send()
+        elif back[i][0]:
+            line_copy(i).wait_send()
+
+
+def fused_shards(residual_stream, grad_output, norm_gain, expert_ids, gate_probs, w_gate, w_up, w_down):
+    experts = lax.axis_size("expert")
+    T = lax.axis_size("tensor")
+    blocks = 2 * T
+    tokens, width = residual_stream.shape
+    hidden = w_gate.shape[1]
+    numbers = jnp.arange(experts, dtype=jnp.int32)
+    onehot = (expert_ids[:, :, None] == numbers[None, None, :]).astype(jnp.int32)
+    named = onehot.sum(axis=1)
+    before = jnp.cumsum(named, axis=0) - named
+    slots = jnp.where(named > 0, before, -1).astype(jnp.float32)
+    probs = jnp.sum(gate_probs[:, :, None] * onehot.astype(jnp.float32), axis=1)
+    meta = jnp.concatenate([slots.T, probs.T], axis=0)
+    gain = jnp.broadcast_to(norm_gain.astype(jnp.float32)[None, :], (8, width))
+    bf16, f32 = jnp.bfloat16, jnp.float32
+    rows = experts * CAP
+    vmem = pl.BlockSpec(memory_space=pltpu.VMEM)
+    hbm = pl.BlockSpec(memory_space=pl.ANY)
+    dma = pltpu.SemaphoreType.DMA
+    unit = (tokens, width)
+    smalls = 3 + 2 * (blocks - 1)
+    return pl.pallas_call(
+        functools.partial(fused_kernel, T),
+        out_shape=jax.ShapeDtypeStruct(unit, bf16),
+        in_specs=[vmem] * 4 + [hbm] * 3,
+        out_specs=vmem,
+        scratch_shapes=[
+            pltpu.VMEM((2, blocks, experts) + unit, bf16),
+            pltpu.VMEM((3, hidden // TILE, rows, TILE), f32),
+            pltpu.VMEM((2, 3, hidden, width), bf16),
+            pltpu.VMEM((2, rows, hidden), bf16),
+            pltpu.VMEM((2, rows, width), bf16),
+            pltpu.VMEM((blocks, 2) + unit, bf16),
+            pltpu.VMEM((blocks,) + unit, bf16),
+            pltpu.VMEM((T,) + unit, bf16),
+            pltpu.VMEM((T - 1,) + unit, bf16),
+            pltpu.VMEM((blocks, 8, width), f32),
+            pltpu.VMEM((experts, 8, tokens), f32),
+            pltpu.VMEM((experts, CAP, tokens), bf16),
+            pltpu.VMEM((rows, 1), f32),
+            pltpu.VMEM((rows, 1), f32),
+            pltpu.VMEM((tokens, 1), f32),
+            pltpu.VMEM((8, tokens), f32),
+            pltpu.VMEM((blocks - 1, 8, tokens), f32),
+            dma((16 * T,)),
+            dma((16 * T,)),
+            dma((blocks, 5)),
+            dma((blocks, 5)),
+            dma((smalls,)),
+            dma((smalls,)),
+            dma((2, 3)),
+            dma((4,)),
+        ],
+        compiler_params=pltpu.CompilerParams(
+            collective_id=0, has_side_effects=True, vmem_limit_bytes=66000000
+        ),
+        name="fused",
+    )(residual_stream, grad_output, gain, meta, w_gate[0], w_up[0], w_down[0])
+
+
 def solution(mesh):
     placed = (
         P("expert", ("tensor", "kv")),
@@ -101,6 +534,9 @@
         P("expert", ("tensor", "kv"), None),
         P("expert", ("tensor", "kv"), None),
     )
+    sizes = dict(mesh.shape)
+    width = D // (sizes["tensor"] * sizes["kv"])
+    body = fused_shards if sizes["expert"] == 4 and sizes["kv"] == 2 and width % 256 == 0 else shards
     return jax.shard_map(
-        shards, mesh=mesh, in_specs=placed, out_specs=P("expert", ("tensor", "kv")), check_vma=False
-    )
+        body, mesh=mesh, in_specs=placed, out_specs=P("expert", ("tensor", "kv")), check_vma=False
+    )

time: 496 us -> 216 us (0.44)
  waiting for transfers between devices: 308 us -> 0 us
  Pallas kernels: 0 us -> 209 us
  matrix products: 89.9 us -> 0 us
  blocking collectives: 69.8 us -> 0 us
  between operations: 13.3 us -> 0.02 us
    pallas_call x0 -> x1, Pallas kernels: none -> 209 us  [fused_shards(): pl.pallas_call(functools.partial(fused_kernel, T), out_shape=jax.ShapeDty...]
    reduce_scatter x1 -> x0, waiting for transfers between devices: 177 us -> none  [shards(): lax.psum_scatter(total + lax.dot_general(up_weight, up_grad, contract_hid...]
    all_gather x2 -> x0, waiting for transfers between devices: 121 us -> none  [the longest x1 71.2 us: shards(): full_x = lax.all_gather(pieces_x, ('tensor', 'kv'), axis=2, tiled=True)]
    dot_general x8 -> x0, matrix products: 89.9 us -> none  [the longest x1 21.7 us: shards(): lax.dot_general(matrix_x, up_weight, contract_width, preferred_element_ty...]
    psum x2 -> x0, blocking collectives: 42.1 us -> none  [the longest x1 22.7 us: shards(): squares = lax.psum(jnp.sum(stream * stream, axis=1), ('tensor', 'kv'))]
    all_to_all x2 -> x0, blocking collectives: 27.7 us -> none  [the longest x1 14.4 us: shards(): lax.all_to_all(routed_grad, 'expert', split_axis=0, concat_axis=0, tiled=...]
    all_to_all x1 -> x0, waiting for transfers between devices: 9.96 us -> none  [shards(): lax.all_to_all(returned, 'expert', split_axis=0, concat_axis=0, tiled=True)]
  transfers between devices with their start and end apart: 4 -> 0, of which waited for: 4 -> 0; matrix products, arithmetic and copies ran while one was open for 4% -> 0% of each run, Pallas kernels for 0% -> 0%
where the time goes in v1:
time: 216 us; the launch traced here: 215 us
  Pallas kernels  209 us (97%)
  other arithmetic  3.34 us (2%)
  local copies, waits for them, and re-layouts  3.25 us (2%)
    pallas_call x1, Pallas kernels, fused_shards(): pl.pallas_call(functools.partial(fused_kernel, T), out_shape=jax.ShapeDty...  209 us

profile of v1, /device:TPU:0, one launch (start us, length us, event | category | flops | bytes accessed | tf_op | source)
XLA Modules:
  0.0 215.3 jit_solution(12966357859280891406)
XLA Ops:
  0.0 0.7 convert_reduce_fusion
  0.7 1.2 reduce-window.6
  1.9 0.1 slice.8
  2.0 0.1 copy.13
  2.1 0.1 copy.14
  2.2 0.1 add_bitcast_fusion
  2.3 0.7 fusion.1
  3.0 0.6 pad_maximum_fusion.meta_ref
  3.6 1.3 broadcast_in_dim.6.gain_ref
  4.9 208.7 %fused.1 = bf16[256,512]{1,0:T(8,128)(2,1)} custom-call(bf16[256,512]{1,0:T(8,128)(2,1)} %x_ref.1, bf16[256,512]{1,0:T(8,128)(2,1)} %dy_ref.1, f32[8,512]{1,0:T(8,128)} %broadcast_in_dim.6.gain_ref, f32[8,256]{1,0:T(8,128)} %pad_maximum_fusion.meta_ref, bf16[1792,4096]{1,0:T(8,128)(2,1)} %bitcast.15, bf16[1792,4096]{1,0:T(8,128)(2,1)} %bitcast.16, ...), custom_call_target="tpu_custom_call" | custom-call | tf_op jit(solution)/shard_map/fused/pallas_call | solution.py:487
  213.7 1.7 copy.18
  (4 shorter events, 0.1 us)

commit v2 on v1

--- a/solution.py
+++ b/solution.py
@@ -102,7 +102,7 @@
     T, x_ref, dy_ref, gain_ref, meta_ref, wg_ref, wu_ref, wd_ref, out_ref,
     tok, acc, wbuf, hid, routed, crecv, xrecv, yrecv, zrecv, gains, metas, sel, prob,
     ssq, own_sq, psend, precv,
-    ag_send, ag_recv, rs_send, rs_recv, small_send, small_recv, wsem, lsem,
+    ag_send, ag_recv, line_send, line_recv, rs_send, rs_recv, small_send, small_recv, wsem, lsem,
 ):
     e = lax.axis_index("expert")
     z = lax.axis_index("tensor")
@@ -118,18 +118,31 @@
     def z_of(d):
         return lax.rem(z + T - d, T)
 
+    nearer_low = z < T - 1 - z
+    reach = jnp.where(nearer_low, z, T - 1 - z)
+
+    def visit(d):
+        if d == 0:
+            return z
+        near = z + (d + 1) // 2 if d % 2 else z - d // 2
+        far = jnp.where(nearer_low, d, T - 1 - d)
+        return jnp.where(d <= 2 * reach, near, far)
+
     def y_of(s):
         return y if s == 0 else 1 - y
 
     def fb_of(d, s):
         return z_of(d) * 2 + y_of(s)
+
+    def seen(d, s):
+        return visit(d) * 2 + y_of(s)
 
     def b_of(u, c):
         base = core if c else e
         return lax.rem(base + 2 * u, 4)
 
     def slot(a, d, s, u, c):
-        return tok.at[a, fb_of(d, s), b_of(u, c)]
+        return tok.at[a, seen(d, s), b_of(u, c)]
 
     def number(a, d, s, u, c):
         return (((a * T + d) * 2 + s) * 2 + u) * 2 + c
@@ -147,12 +160,12 @@
                 return (d, 0, u, 0), (e, z, 1 - y)
             if u:
                 return (d, 0, 0, 0), (across, z, y)
-        return (0, 0, 0, 0), (e, lax.rem(z + d, T), y)
+        raise ValueError(d)
 
     def gather_copy(a, d, s, u, c):
         source, target = plan(a, d, s, u, c)
         n = number(a, d, s, u, c)
-        fb, b = fb_of(*source[:2]), b_of(*source[2:])
+        fb, b = seen(*source[:2]), b_of(*source[2:])
         src = inputs[a] if source == (0, 0, 0, 0) else tok.at[a, fb, b]
         return pltpu.make_async_remote_copy(
             src_ref=src, dst_ref=tok.at[a, fb, b],
@@ -173,7 +186,7 @@
 
     def weight_copies(step):
         if step < blocks:
-            fb, refs = fb_of(*steps[step]), (wg_ref, wu_ref, wd_ref)
+            fb, refs = seen(*steps[step]), (wg_ref, wu_ref, wd_ref)
         else:
             fb, refs = fb_of(*back[step - blocks]), (wg_ref, wu_ref)
         columns = pl.ds(pl.multiple_of(fb * width, width), width)
@@ -213,9 +226,39 @@
         copy.start()
         there = metas.at[lax.rem(e + 3 - k, 4)]
         small.append((copy, remote(there, there, small_send.at[k], small_recv.at[k], peer)))
-    for d in range(1, T):
-        for a in (0, 1):
-            gather_copy(a, d, 0, 0, 0).start()
+
+    def own_line(a, way):
+        fb = fb_of(0, 0)
+        return remote(
+            inputs[a], tok.at[a, fb, e], line_send.at[a, way], line_recv.at[a, z],
+            (e, z + 2 * way - 1, y),
+        )
+
+    def pass_on(a, d):
+        v = visit(d)
+        here = tok.at[a, seen(d, 0), e]
+        return remote(
+            here, here, line_send.at[a, 1 + d], line_recv.at[a, v],
+            (e, jnp.where(v < z, z + 1, z - 1), y),
+        )
+
+    def passes(d):
+        v = visit(d)
+        return jnp.where(v < z, z < T - 1, z > 0)
+
+    for a in (0, 1):
+        for way in (0, 1):
+            @pl.when(z < T - 1 if way else z > 0)
+            def _():
+                own_line(a, way).start()
+
+    def arrive(a, d):
+        pass_on(a, d).wait_recv()
+
+        @pl.when(passes(d))
+        def _():
+            pass_on(a, d).start()
+
     for k, peer in enumerate(peers):
         n = 3 + k
         copy = remote(gain_ref, gains.at[fb_of(0, 0)], small_send.at[n], small_recv.at[n], peer)
@@ -225,14 +268,14 @@
 
     def level1(d):
         if d:
-            gather_wait(0, d, 0, 0, 0)
+            arrive(0, d)
         gather_copy(0, d, 1, 0, 0).start()
+        if d:
+            arrive(1, d)
+        gather_copy(1, d, 0, 1, 0).start()
         gather_copy(0, d, 0, 1, 0).start()
+        gather_copy(1, d, 1, 0, 0).start()
         gather_copy(0, d, 0, 0, 1).start()
-        if d:
-            gather_wait(1, d, 0, 0, 0)
-        gather_copy(1, d, 0, 1, 0).start()
-        gather_copy(1, d, 1, 0, 0).start()
         gather_copy(1, d, 0, 0, 1).start()
 
     def level2(d):
@@ -260,7 +303,7 @@
         for a in (0, 1):
             for u in (0, 1):
                 gather_wait(a, d, s, u, 1)
-        fb = fb_of(d, s)
+        fb = seen(d, s)
         gain_row = gains[fb, 0:1, :]
         mine = tok[0, fb, e].astype(jnp.float32)
         own_sq[...] += jnp.sum(mine * mine, axis=1, keepdims=True)
@@ -290,6 +333,7 @@
         lax.fori_loop(0, tiles, tile, 0)
 
     level1(0)
+    level2(0)
     for copy in local:
         copy.wait()
     for copy, arrival in small[:3]:
@@ -306,26 +350,34 @@
     for copy, arrival in small[3:]:
         arrival.wait_recv()
     level1(1)
-    level2(0)
+    level3(0)
+    multiply(0)
+    level2(1)
     level1(2)
-    level3(0)
-    level2(1)
-    level1(3)
-    multiply(0)
+    for d in range(3, T):
+        level1(d)
+    multiply(1)
     level3(1)
-    level2(2)
-    multiply(1)
-    level2(3)
-    level3(2)
-    multiply(2)
-    multiply(3)
-    level3(3)
-    for step in range(4, blocks):
-        multiply(step)
+    for d in range(2, T):
+        multiply(2 * d - 2)
+        level2(d)
+        multiply(2 * d - 1)
+        level3(d)
+    multiply(blocks - 2)
+    multiply(blocks - 1)
     for a in (0, 1):
         for n in range(1, blocks * 4):
             c, u, s, d = n % 2, n // 2 % 2, n // 4 % 2, n // 8
-            gather_copy(a, d, s, u, c).wait_send()
+            if s or u or c:
+                gather_copy(a, d, s, u, c).wait_send()
+        for way in (0, 1):
+            @pl.when(z < T - 1 if way else z > 0)
+            def _():
+                own_line(a, way).wait_send()
+        for d in range(1, T):
+            @pl.when(passes(d))
+            def _():
+                pass_on(a, d).wait_send()
     for copy, arrival in small:
         copy.wait_send()
 
@@ -509,6 +561,8 @@
             pltpu.VMEM((blocks - 1, 8, tokens), f32),
             dma((16 * T,)),
             dma((16 * T,)),
+            dma((2, T + 1)),
+            dma((2, T)),
             dma((blocks, 5)),
             dma((blocks, 5)),
             dma((smalls,)),

time: 216 us -> 173 us (0.80)
  Pallas kernels: 209 us -> 166 us
    pallas_call x1, Pallas kernels: 209 us -> 166 us  [fused_shards(): pl.pallas_call(functools.partial(fused_kernel, T), out_shape=jax.ShapeDty...]
where the time goes in v2:
time: 173 us; the launch traced here: 172 us
  Pallas kernels  166 us (96%)
  other arithmetic  3.34 us (2%)
  local copies, waits for them, and re-layouts  3.25 us (2%)
    pallas_call x1, Pallas kernels, fused_shards(): pl.pallas_call(functools.partial(fused_kernel, T), out_shape=jax.ShapeDty...  166 us

profile of v2, /device:TPU:0, one launch (start us, length us, event | category | flops | bytes accessed | tf_op | source)
XLA Modules:
  0.0 172.3 jit_solution(2180676208821561695)
XLA Ops:
  0.0 0.7 convert_reduce_fusion
  0.7 1.2 reduce-window.6
  1.9 0.1 slice.8
  2.0 0.1 copy.13
  2.1 0.1 copy.14
  2.2 0.1 add_bitcast_fusion
  2.3 0.7 fusion.1
  3.0 0.6 pad_maximum_fusion.meta_ref
  3.6 1.3 broadcast_in_dim.6.gain_ref
  4.9 165.7 %fused.1 = bf16[256,512]{1,0:T(8,128)(2,1)} custom-call(bf16[256,512]{1,0:T(8,128)(2,1)} %x_ref.1, bf16[256,512]{1,0:T(8,128)(2,1)} %dy_ref.1, f32[8,512]{1,0:T(8,128)} %broadcast_in_dim.6.gain_ref, f32[8,256]{1,0:T(8,128)} %pad_maximum_fusion.meta_ref, bf16[1792,4096]{1,0:T(8,128)(2,1)} %bitcast.15, bf16[1792,4096]{1,0:T(8,128)(2,1)} %bitcast.16, ...), custom_call_target="tpu_custom_call" | custom-call | tf_op jit(solution)/shard_map/fused/pallas_call | solution.py:539
  170.7 1.7 copy.18
  (4 shorter events, 0.1 us)

commit v3 on v2

--- a/solution.py
+++ b/solution.py
@@ -359,8 +359,12 @@
     multiply(1)
     level3(1)
     for d in range(2, T):
-        multiply(2 * d - 2)
-        level2(d)
+        if d == 2:
+            level2(d)
+            multiply(2 * d - 2)
+        else:
+            multiply(2 * d - 2)
+            level2(d)
         multiply(2 * d - 1)
         level3(d)
     multiply(blocks - 2)

time: 173 us -> 174 us (level)
  no operation moved by 1% of the time
where the time goes in v3:
time: 174 us
  Pallas kernels  167 us (96%)
  other arithmetic  3.34 us (2%)
  local copies, waits for them, and re-layouts  3.25 us (2%)
    pallas_call x1, Pallas kernels, fused_shards(): pl.pallas_call(functools.partial(fused_kernel, T), out_shape=jax.ShapeDty...  167 us

profile of v3, /device:TPU:0, one launch (start us, length us, event | category | flops | bytes accessed | tf_op | source)
XLA Modules:
  0.0 173.6 jit_solution(7469304056480698401)
XLA Ops:
  0.0 0.7 convert_reduce_fusion
  0.7 1.2 reduce-window.6
  1.9 0.1 slice.8
  2.0 0.1 copy.13
  2.1 0.1 copy.14
  2.2 0.1 add_bitcast_fusion
  2.3 0.7 fusion.1
  3.0 0.6 pad_maximum_fusion.meta_ref
  3.6 1.3 broadcast_in_dim.6.gain_ref
  4.9 167.0 %fused.1 = bf16[256,512]{1,0:T(8,128)(2,1)} custom-call(bf16[256,512]{1,0:T(8,128)(2,1)} %x_ref.1, bf16[256,512]{1,0:T(8,128)(2,1)} %dy_ref.1, f32[8,512]{1,0:T(8,128)} %broadcast_in_dim.6.gain_ref, f32[8,256]{1,0:T(8,128)} %pad_maximum_fusion.meta_ref, bf16[1792,4096]{1,0:T(8,128)(2,1)} %bitcast.15, bf16[1792,4096]{1,0:T(8,128)(2,1)} %bitcast.16, ...), custom_call_target="tpu_custom_call" | custom-call | tf_op jit(solution)/shard_map/fused/pallas_call | solution.py:543
  172.0 1.7 copy.18
  (4 shorter events, 0.1 us)
